TPU v7x, 256 devices: a whole 4x4x8 slice. The times are simulated.
256 devices in a mesh: seq: 32 (over y, x, core), tp: 8 (over z).
Axes of the slice: x: 4, y: 4, z: 8, core: 2. Of those that a mesh axis runs over, the one named last changes fastest.
Arguments:
- queries: bfloat16 [32, 64, 4096], P('seq', None, 'tp'), may hold values from -8 to 8
- draft_kv: bfloat16 [32, 64, 8, 128], P('seq', None, 'tp'), may hold values from -12.5 to 12.5
- cache_kv: bfloat16 [8, 16384, 8, 128], P(None, 'seq', 'tp'), may hold values from -10 to 10
- cache_len: int32 [8], replicated, may hold values from 4096 to 16384
- group_of: int32 [32], replicated, may hold values from 0 to 7, as said below
- parents: int32 [32, 64], P('seq'), may hold values from 0 to 62, as said below
- sink_logit: float32 [64], P('tp'), may hold values from 4 to 20
- w_out: bfloat16 [4096, 2880], P('tp'), may hold values from -0.09375 to 0.09375
- hidden_in: bfloat16 [2048, 2880], P('seq', 'tp'), may hold values from -3 to 3
- norm_gain: float32 [2880], replicated, may hold values from 0.5 to 1.5
- routes: int32 [2048, 4], P('seq'), may hold values from 0 to 31, all different within a row; in each aligned block of 64 rows (0 to 63, 64 to 127, ...) at most 16 rows name the same one
- route_weight: float32 [2048, 4], P('seq'), may hold values from 0.1 to 1
- w_gate_up: bfloat16 [32, 2, 2880, 2880], P('seq', None, None, 'tp'), may hold values from -0.109375 to 0.109375
- w_down: bfloat16 [32, 2880, 2880], P('seq', 'tp'), may hold values from -0.109375 to 0.109375
- accepted_idx: int32 [32, 16], P('seq'), may hold values from 0 to 45, as said below
- accepted_len: int32 [32], P('seq'), may hold values from 1 to 16, as said below
- tail_slot: int32 [32], replicated, may hold values from 0 to 31, each once
Outputs:
- out_hidden: bfloat16 [2048, 2880], P('seq', 'tp')
- new_tail: bfloat16 [32, 16, 8, 128], P('seq', None, 'tp')
Inputs may be any that keep to these rules, and one draw needn't show every extreme that they name: `parents`: node 0 of every tree is its root and its own parent; every other node's parent is one of the three nodes before it. `accepted_idx`: row r lists the first 16 nodes of a path from the root of request r's tree down to one of its last four nodes, root first. `accepted_len`: each request accepts one or more nodes. `group_of`: every prompt group has exactly 4 requests. `routes`: the 4 experts of a token differ; at most 16 of one device's rows (one aligned block of 64 tokens) name one expert.
All inputs are finite; a program needn't handle non-finite values.
Results may differ from a plain program's by a relative error of at most 0.025.
Values may be sent and summed in bfloat16 or wider, within the bound.
A program may use at most 128 MiB of HBM per device.

v0:
```python
import jax
import jax.numpy as jnp
from jax import lax
from jax.sharding import PartitionSpec as P

HQ = 64
KVH = 8
HD = 64


def ancestry(parents):
    tree_len = parents.shape[1]
    node_ids = jnp.arange(tree_len, dtype=jnp.int32)
    linked = (parents[:, :, None] == node_ids[None, None, :]) | (
        node_ids[:, None] == node_ids[None, :]
    )[None]
    reachable = linked.astype(jnp.float32)
    for repeat in range((tree_len - 1).bit_length()):
        reachable = jnp.minimum(
            jnp.einsum("rij,rjk->rik", reachable, reachable, precision=lax.Precision.HIGHEST), 1.0
        )
    return reachable


def cache_block(block_queries, block_groups, cache_kv, cache_len, positions):
    block_rows, tree_len, head_cols = block_queries.shape
    kv_dev = cache_kv.shape[2]
    grouped = block_queries.reshape(block_rows, tree_len, kv_dev, HQ // KVH, HD)
    picked = jnp.take(cache_kv, block_groups, axis=0)
    cache_keys = picked[..., :HD]
    cache_values = picked[..., HD:]
    scores = (
        jnp.einsum("rtkqd,rckd->rkqtc", grouped, cache_keys, preferred_element_type=jnp.float32)
        * 0.125
    )
    lengths = jnp.take(cache_len, block_groups)
    usable = (positions[None, :] < lengths[:, None])[:, None, None, None, :]
    masked = jnp.where(usable, scores, -1e30)
    shard_max = jnp.max(masked, axis=-1)
    weights = jnp.where(usable, jnp.exp(masked - shard_max[..., None]), 0.0)
    shard_sum = jnp.sum(weights, axis=-1)
    shard_out = jnp.einsum(
        "rkqtc,rckd->rkqtd",
        weights.astype(jnp.bfloat16),
        cache_values,
        preferred_element_type=jnp.float32,
    )
    shard_out = (shard_out / jnp.maximum(shard_sum, 1.0)[..., None]).astype(jnp.bfloat16)
    out_rows = shard_out.transpose(0, 3, 1, 2, 4).reshape(block_rows, tree_len, head_cols)
    max_rows = shard_max.transpose(0, 3, 1, 2).reshape(block_rows, tree_len, -1)
    sum_rows = shard_sum.transpose(0, 3, 1, 2).reshape(block_rows, tree_len, -1)
    return (out_rows, max_rows, sum_rows)


def expert_rows(arrived, w_gate_up, w_down):
    exp_dev = w_gate_up.shape[0]
    sources = arrived.shape[0] // exp_dev
    grouped = arrived.reshape(sources, exp_dev, arrived.shape[1], arrived.shape[2])
    gate_proj = jnp.einsum(
        "sexd,edf->sexf", grouped, w_gate_up[:, 0], preferred_element_type=jnp.float32
    )
    upward = jnp.einsum(
        "sexd,edf->sexf", grouped, w_gate_up[:, 1], preferred_element_type=jnp.float32
    )
    active = (gate_proj * jax.nn.sigmoid(1.702 * gate_proj) * (upward + 1.0)).astype(jnp.bfloat16)
    down_part = jnp.einsum("sexf,efd->sexd", active, w_down, preferred_element_type=jnp.float32)
    return down_part.reshape(arrived.shape[0], arrived.shape[1], -1)


def shards(
    queries,
    draft_kv,
    cache_kv,
    cache_len,
    group_of,
    parents,
    sink_logit,
    w_out,
    hidden_in,
    norm_gain,
    routes,
    route_weight,
    w_gate_up,
    w_down,
    accepted_idx,
    accepted_len,
    tail_slot,
):
    seq_count = lax.axis_size("seq")
    req_dev, tree_len, head_cols = queries.shape
    kv_dev = cache_kv.shape[2]
    per_kv = HQ // KVH
    heads_dev = kv_dev * per_kv
    shard_len = cache_kv.shape[1]
    positions = lax.axis_index("seq") * shard_len + jnp.arange(shard_len, dtype=jnp.int32)
    every_query = lax.all_gather(queries, "seq", axis=0, tiled=True)
    requests_all = every_query.shape[0]
    block_count = requests_all // 8
    stacked = (
        every_query.reshape(block_count, 8, tree_len, head_cols),
        group_of.reshape(block_count, 8),
    )
    shard_out, shard_max, shard_sum = lax.map(
        lambda blocks: cache_block(blocks[0], blocks[1], cache_kv, cache_len, positions), stacked
    )
    shard_out = shard_out.reshape(seq_count, req_dev, tree_len, head_cols)
    shard_max = shard_max.reshape(seq_count, req_dev, tree_len, heads_dev)
    shard_sum = shard_sum.reshape(seq_count, req_dev, tree_len, heads_dev)
    came_out = lax.all_to_all(shard_out, "seq", split_axis=0, concat_axis=0, tiled=True)
    came_max, came_sum = (
        lax.all_to_all(shard_max, "seq", split_axis=0, concat_axis=0, tiled=True),
        lax.all_to_all(shard_sum, "seq", split_axis=0, concat_axis=0, tiled=True),
    )
    reachable = ancestry(parents)
    own_heads = queries.reshape(req_dev, tree_len, kv_dev, per_kv, HD)
    draft_keys = draft_kv[..., :HD]
    draft_values = draft_kv[..., HD:]
    tree_scores = (
        jnp.einsum("rtkqd,rukd->rkqtu", own_heads, draft_keys, preferred_element_type=jnp.float32)
        * 0.125
    )
    allowed = (reachable > 0.5)[:, None, None, :, :]
    tree_masked = jnp.where(allowed, tree_scores, -1e30)
    tree_max = jnp.max(tree_masked, axis=-1)
    tree_weight = jnp.where(allowed, jnp.exp(tree_masked - tree_max[..., None]), 0.0)
    tree_sum = jnp.sum(tree_weight, axis=-1)
    tree_num = jnp.einsum(
        "rkqtu,rukd->rkqtd",
        tree_weight.astype(jnp.bfloat16),
        draft_values,
        preferred_element_type=jnp.float32,
    )
    tree_max = tree_max.transpose(0, 3, 1, 2).reshape(req_dev, tree_len, heads_dev)
    tree_sum = tree_sum.transpose(0, 3, 1, 2).reshape(req_dev, tree_len, heads_dev)
    tree_num = tree_num.transpose(0, 3, 1, 2, 4).reshape(req_dev, tree_len, heads_dev, HD)
    sink_rows = sink_logit[None, None, :]
    ceiling = jnp.maximum(jnp.maximum(jnp.max(came_max, axis=0), tree_max), sink_rows)
    shard_scale = came_sum * jnp.exp(came_max - ceiling[None])
    tree_scale = jnp.exp(tree_max - ceiling)
    denominator = (
        jnp.sum(shard_scale, axis=0) + tree_scale * tree_sum + jnp.exp(sink_rows - ceiling)
    )
    weighted = jnp.sum(
        shard_scale[..., None]
        * came_out.reshape(seq_count, req_dev, tree_len, heads_dev, HD).astype(jnp.float32),
        axis=0,
    )
    numerator = weighted + tree_scale[..., None] * tree_num
    attention = (
        (numerator / denominator[..., None])
        .reshape(req_dev * tree_len, heads_dev * HD)
        .astype(jnp.bfloat16)
    )
    projected = jnp.dot(attention, w_out, preferred_element_type=jnp.float32)
    width_dev = hidden_in.shape[1]
    tp_index = lax.axis_index("tp")
    summed = lax.psum(projected, "tp")
    resid_full = lax.all_gather(hidden_in, "tp", axis=1, tiled=True)
    stream = (resid_full.astype(jnp.float32) + summed).astype(jnp.bfloat16)
    stream_f = stream.astype(jnp.float32)
    inv_scale = lax.rsqrt(jnp.mean(stream_f * stream_f, axis=-1, keepdims=True) + 1e-05)
    normed_full = (stream_f * inv_scale * norm_gain[None, :]).astype(jnp.bfloat16)
    stream_cols = lax.dynamic_slice_in_dim(stream, tp_index * width_dev, width_dev, 1)
    tok_dev = routes.shape[0]
    top_count = routes.shape[1]
    exp_dev = w_gate_up.shape[0]
    experts_all = seq_count * exp_dev
    capacity = 2 * tok_dev * top_count // experts_all
    flat_routes = routes.reshape(-1)
    onehot = (flat_routes[:, None] == jnp.arange(experts_all, dtype=jnp.int32)[None, :]).astype(
        jnp.int32
    )
    position = jnp.sum((jnp.cumsum(onehot, axis=0) - onehot) * onehot, axis=1)
    slot_ids = flat_routes * capacity + position
    buckets = jnp.arange(experts_all * capacity, dtype=jnp.int32)
    placing = jnp.sum(
        (slot_ids.reshape(tok_dev, top_count)[None, :, :] == buckets[:, None, None]).astype(
            jnp.int32
        ),
        axis=2,
    ).astype(jnp.bfloat16)
    dispatched = (
        jnp.dot(placing, normed_full, preferred_element_type=jnp.float32)
        .astype(jnp.bfloat16)
        .reshape(experts_all, capacity, -1)
    )
    down_part = expert_rows(
        lax.all_to_all(dispatched, "seq", split_axis=0, concat_axis=0, tiled=True),
        w_gate_up,
        w_down,
    )
    expert_out = lax.psum_scatter(
        down_part.astype(jnp.bfloat16), "tp", scatter_dimension=2, tiled=True
    )
    returned = lax.all_to_all(expert_out, "seq", split_axis=0, concat_axis=0, tiled=True)
    gathered_rows = jnp.take(
        returned.reshape(experts_all * capacity, -1), slot_ids, axis=0
    ).reshape(tok_dev, top_count, -1)
    mixture = jnp.sum(route_weight[:, :, None] * gathered_rows.astype(jnp.float32), axis=1)
    out_hidden = (stream_cols.astype(jnp.float32) + mixture).astype(jnp.bfloat16)
    blk_len = accepted_idx.shape[1]
    chosen = draft_kv[jnp.arange(req_dev, dtype=jnp.int32)[:, None], accepted_idx]
    kept_rows = jnp.arange(blk_len, dtype=jnp.int32)[None, :] < accepted_len[:, None]
    picked_rows = jnp.where(kept_rows[:, :, None, None], chosen, jnp.zeros_like(chosen))
    everyone = lax.all_gather(picked_rows, "seq", axis=0, tiled=True)
    my_slots = lax.axis_index("seq") * req_dev + jnp.arange(req_dev, dtype=jnp.int32)
    selector = (tail_slot[None, :] == my_slots[:, None]).astype(jnp.bfloat16)
    new_tail = jnp.dot(
        selector, everyone.reshape(everyone.shape[0], -1), preferred_element_type=jnp.float32
    ).astype(jnp.bfloat16)
    new_tail = new_tail.reshape(req_dev, blk_len, kv_dev, -1)
    return (out_hidden, new_tail)


def solution(mesh):
    in_specs = (
        P("seq", None, "tp"),
        P("seq", None, "tp", None),
        P(None, "seq", "tp", None),
        P(),
        P(),
        P("seq", None),
        P("tp"),
        P("tp", None),
        P("seq", "tp"),
        P(),
        P("seq", None),
        P("seq", None),
        P("seq", None, None, "tp"),
        P("seq", "tp", None),
        P("seq", None),
        P("seq"),
        P(),
    )
    out_specs = (P("seq", "tp"), P("seq", None, "tp", None))
    return jax.shard_map(shards, mesh=mesh, in_specs=in_specs, out_specs=out_specs, check_vma=False)
```

profile of v0, /device:TPU:1, one launch (start us, length us, event | category | flops | bytes accessed | tf_op | source)
XLA Modules:
  0.0 533.3 jit_solution(3878875501359007208)
XLA Ops:
  8.8 1.5 convolution_minimum_fusion.5
  10.3 53.3 %all-gather.3.cloned.1.call-done = bf16[32,64,512]{2,1,0:T(8,128)(2,1)} async-done(((bf16[1,64,512]{2,1,0:T(8,128)(2,1)}), bf16[32,64,512]{2,1,0:T(8,128)(2,1)}) %all-gather.3.cloned.1.call-update) | async-done | bytes 2097168 | tf_op jit(solution)/shard_map/all_gather | solution.py:96
  63.7 97.3 %while.15 = (s32[]{:T(128)}, bf16[4,8,64,512]{3,2,1,0:T(8,128)(2,1)}, f32[4,8,64,8]{2,3,1,0:T(8,128)}, f32[4,8,64,8]{2,3,1,0:T(8,128)}, s32[4,8]{1,0:T(4,128)S(1...) while((s32[]{:T(128)}, ...), condition=%wide.region_3.4_spmd.clone, body=%wide.region_0.3_spmd.clone.sunk | while | flops 565184128 | bytes 43791872 | solution.py:103
  65.0 2.9 gather_fusion.1
  67.9 2.3 copy.129
  70.2 2.4 bitcast_select_fusion.4
  75.3 2.7 bitcast_reduce_fusion.3
  78.0 2.3 fusion.128
  80.9 2.6 fusion.129
  83.6 1.7 copy.130
  85.3 1.9 broadcast_in_dim.201
  89.4 2.9 gather_fusion.1
  92.3 2.3 copy.129
  94.5 2.4 bitcast_select_fusion.4
  99.6 2.7 bitcast_reduce_fusion.3
  102.3 2.3 fusion.128
  105.3 2.6 fusion.129
  107.9 1.7 copy.130
  109.6 1.9 broadcast_in_dim.201
  113.7 2.9 gather_fusion.1
  116.6 2.3 copy.129
  118.9 2.4 bitcast_select_fusion.4
  124.0 2.7 bitcast_reduce_fusion.3
  126.7 2.3 fusion.128
  129.6 2.6 fusion.129
  132.2 1.7 copy.130
  133.9 1.9 broadcast_in_dim.201
  138.0 2.9 gather_fusion.1
  140.9 2.3 copy.129
  143.2 2.4 bitcast_select_fusion.4
  148.3 2.7 bitcast_reduce_fusion.3
  151.0 2.3 fusion.128
  153.9 2.6 fusion.129
  156.5 1.7 copy.130
  158.2 1.9 broadcast_in_dim.201
  161.0 1.7 reshape.754
  162.7 5.1 all-to-all-start.1
  168.8 1.7 reshape.752
  170.4 4.7 all-to-all-done.1
  175.1 3.9 all-to-all-start
  180.8 5.6 %all-to-all-done = f32[32,1,512]{2,1,0:T(1,128)S(1)} async-done(((f32[32,1,512]{2,1,0:T(1,128)}), f32[32,1,512]{2,1,0:T(1,128)S(1)}, u32[]{:S(2)}, u32[]{:S(2)}) %all-to-all-start) | async-done | bytes 65568 | tf_op jit(solution)/shard_map/all_to_all | solution.py:112
  186.4 4.7 all-to-all-start.2
  193.3 23.3 %all-gather = bf16[8,360,64]{1,2,0:T(8,128)(2,1)S(1)} all-gather(bf16[1,360,64]{1,2,0:T(8,128)(2,1)} %bitcast.318), channel_id=1, replica_groups=mesh['seq'=32,'tp'=8] {'tp'}, dimensions={0}, use_global_device_ids=true | all-gather | bytes 414720 | tf_op jit(solution)/shard_map/all_gather | solution.py:158
  217.7 2.3 reshape.728
  227.4 5.9 %mul.135 = f32[32,64,8,64]{3,2,1,0:T(8,128)} broadcast(f32[32,64,8]{2,1,0:T(8,128)} %copy.92), dimensions={0,1,2} | broadcast | bytes 4259840 | tf_op jit(solution)/shard_map/mul | solution.py:144
  233.4 7.5 %mul.136 = f32[32,1,64,512]{3,2,1,0:T(8,128)} reshape(f32[32,64,8,64]{3,2,1,0:T(8,128)} %mul.135) | data formatting | bytes 8388608 | tf_op jit(solution)/shard_map/mul | solution.py:144
  240.9 3.6 multiply_reduce_fusion
  244.5 1.9 fusion.77
  247.8 72.6 %all-reduce.3.cloned.1.call-done = f32[64,2880]{1,0:T(8,128)} async-done(((f32[64,2880]{1,0:T(8,128)}), f32[64,2880]{1,0:T(8,128)}) %all-reduce.3.cloned.1.call-update) | async-done | bytes 737296 | tf_op jit(solution)/shard_map/psum | solution.py:157
  322.7 2.7 convolution_convert_fusion.1
  325.4 4.6 copy.103
  329.9 50.3 %all_to_all.25 = bf16[32,16,2880]{2,1,0:T(8,128)(2,1)S(1)} all-to-all(bf16[32,16,2880]{2,1,0:T(8,128)(2,1)} %bitcast.309), channel_id=1, replica_groups=mesh['seq'=32,'tp'=8] {'seq'}, dimensions={0} | all-to-all | bytes 5898240 | tf_op jit(solution)/shard_map/all_to_all | solution.py:188
  380.2 1.6 copy-done.2
  381.9 4.2 fusion.27
  386.1 8.5 %convolution_convert_fusion = bf16[32,16,2880]{2,1,0:T(8,128)(2,1)} fusion(bf16[1,360,2880]{2,1,0:T(8,128)(2,1)} %param.32, bf16[32,16,2880]{2,1,0:T(8,128)(2,1)} %copy-done.2, bf16[1,2,2880,360]{2,3,1,0:T(8,128)(2,1)} %param.31, f32[32,1,16,360]{3,2,0,1:T(8,128)} %fusion.27), kind=kOutput, calls=%fused_computation.40 | convolution fusion | flops 2126315520 | bytes 10989568 | tf_op jit(solution)/shard_map/sexf,efd->sexd/dot_general | solution.py:66
  394.6 21.4 %copy.108 = bf16[32,16,2880]{1,0,2:T(8,128)(2,1)} copy(bf16[32,16,2880]{2,1,0:T(8,128)(2,1)} %convolution_convert_fusion) | data formatting | bytes 5898240
  416.0 39.5 %reshape.749 = bf16[2880,512]{1,0:T(8,128)(2,1)} reshape(bf16[2880,32,16]{2,1,0:T(8,128)(2,1)} %bitcast.306) | data formatting | bytes 5898240
  457.1 22.6 %all_gather.11 = bf16[32,16,1,128]{3,1,2,0:T(8,128)(2,1)S(1)} all-gather(bf16[1,16,1,128]{3,1,2,0:T(8,128)(2,1)S(1)} %bitcast_select_fusion.2), channel_id=1, replica_groups=mesh['seq'=32,'tp'=8] {'seq'}, dimensions={0}, use_global_device_ids=true | all-gather | bytes 135168 | tf_op jit(solution)/shard_map/all_gather | solution.py:205
  479.9 12.3 %reduce-scatter.4.cloned.1.call-done = bf16[360,512]{1,0:T(8,128)(2,1)} async-done(((bf16[2880,512]{1,0:T(8,128)(2,1)}), bf16[360,512]{1,0:T(8,128)(2,1)}) %reduce-scatter.4.cloned.1.call-update) | async-done | bytes 368656
  492.2 4.4 reshape.750
  496.5 5.0 copy.109
  501.6 11.1 %all-to-all-start.4 = ((bf16[32,16,360]{2,1,0:T(8,128)(2,1)}), bf16[32,16,360]{2,1,0:T(8,128)(2,1)S(1)}, u32[]{:S(2)}, u32[]{:S(2)}) async-start(bf16[32,16,360]{2,1,0:T(8,128)(2,1)} %copy.109), calls=%async_computation.4 | async-start | bytes 786432 | tf_op jit(solution)/shard_map/all_to_all | solution.py:195
  514.1 8.7 %all-to-all-done.4 = bf16[32,16,360]{2,1,0:T(8,128)(2,1)S(1)} async-done(((bf16[32,16,360]{2,1,0:T(8,128)(2,1)}), bf16[32,16,360]{2,1,0:T(8,128)(2,1)S(1)}, u32[]{:S(2)}, u32[]{:S(2)}) %all-to-all-start.4) | async-done | bytes 368672 | tf_op jit(solution)/shard_map/all_to_all | solution.py:195
  525.2 1.6 add_convert_fusion
  (162 shorter events, 45.4 us)
Async XLA Ops:
  7.2 237.3 %copy-start = (bf16[512,2880]{0,1:T(8,128)(2,1)S(1)}, bf16[512,2880]{0,1:T(8,128)(2,1)}, u32[]{:S(2)}) copy-start(bf16[512,2880]{0,1:T(8,128)(2,1)} %param.26) | copy-start | bytes 8847364
  7.2 56.5 %all-gather.3.cloned.1.call-start = ((), (), s32[]{:S(2)}) async-start(), calls=%async_computation.6 | async-start | bytes 2162688 | tf_op jit(solution)/shard_map/all_gather | solution.py:96
  63.7 115.5 %copy-start.6 = (bf16[1,64,512]{2,1,0:T(8,128)(2,1)S(1)}, bf16[1,64,512]{2,1,0:T(8,128)(2,1)}, u32[]{:S(2)}) copy-start(bf16[1,64,512]{2,1,0:T(8,128)(2,1)} %param.19) | copy-start | bytes 196612
  63.7 115.6 %copy-start.13 = (s32[64,4]{0,1:T(4,128)S(1)}, s32[64,4]{0,1:T(4,128)}, u32[]{:S(2)}) copy-start(s32[64,4]{0,1:T(4,128)} %param.29) | copy-start | bytes 3076
  78.0 3.0 copy-start.1
  102.3 3.0 copy-start.1
  126.6 3.0 copy-start.1
  150.9 3.0 copy-start.1
  161.0 30.9 %copy-start.7 = (bf16[1,64,1,128]{3,1,2,0:T(8,128)(2,1)S(1)}, bf16[1,64,1,128]{3,1,2,0:T(8,128)(2,1)}, u32[]{:S(2)}) copy-start(bf16[1,64,1,128]{3,1,2,0:T(8,128)(2,1)} %param.20) | copy-start | bytes 49156
  162.7 12.4 %all-to-all-start.1 = ((f32[32,1,512]{2,1,0:T(1,128)}), f32[32,1,512]{2,1,0:T(1,128)S(1)}, u32[]{:S(2)}, u32[]{:S(2)}) async-start(f32[32,1,512]{2,1,0:T(1,128)} %reshape.754), calls=%async_computation.1 | async-start | bytes 131072 | tf_op jit(solution)/shard_map/all_to_all | solution.py:111
  175.1 17.0 %copy-start.9 = (f32[32,1,512]{2,1,0:T(1,128)}, f32[32,1,512]{2,1,0:T(1,128)S(1)}, u32[]{:S(2)}) copy-start(f32[32,1,512]{2,1,0:T(1,128)S(1)} %all-to-all-done.1) | copy-start | bytes 196612
  175.1 11.3 %all-to-all-start = ((f32[32,1,512]{2,1,0:T(1,128)}), f32[32,1,512]{2,1,0:T(1,128)S(1)}, u32[]{:S(2)}, u32[]{:S(2)}) async-start(f32[32,1,512]{2,1,0:T(1,128)} %reshape.752), calls=%async_computation | async-start | bytes 131072 | tf_op jit(solution)/shard_map/all_to_all | solution.py:112
  186.4 4.8 copy-start.11
  186.4 54.4 %all-to-all-start.2 = ((bf16[32,1,64,512]{3,2,1,0:T(8,128)(2,1)}), bf16[32,1,64,512]{3,2,1,0:T(8,128)(2,1)}, u32[]{:S(2)}, u32[]{:S(2)}) async-start(bf16[32,1,64,512]{3,2,1,0:T(8,128)(2,1)} %bitcast.313), calls=%async_computation.2 | async-start | bytes 4194304 | tf_op jit(solution)/shard_map/all_to_all | solution.py:109
  191.2 129.2 %all-reduce.3.cloned.1.call-start = ((), (), s32[]{:S(2)}) async-start(), calls=%async_computation.7 | async-start | bytes 1507328 | tf_op jit(solution)/shard_map/psum | solution.py:157
  192.4 28.8 %copy-start.10 = (f32[32,1,512]{2,1,0:T(1,128)S(1)}, f32[32,1,512]{2,1,0:T(1,128)}, u32[]{:S(2)}) copy-start(f32[32,1,512]{2,1,0:T(1,128)} %copy-done.9) | copy-start | bytes 196612
  193.3 28.8 %copy-start.12 = (f32[32,1,512]{2,1,0:T(1,128)S(1)}, f32[32,1,512]{2,1,0:T(1,128)}, u32[]{:S(2)}) copy-start(f32[32,1,512]{2,1,0:T(1,128)} %copy-done.11) | copy-start | bytes 196612
  240.9 3.6 copy-start.4
  240.9 3.6 copy-start.5
  244.5 2.0 copy-start.16
  244.5 2.8 copy-start.15
  244.5 78.2 %copy-start.14 = (f32[2880]{0:T(1024)S(1)}, f32[2880]{0:T(1024)}, u32[]{:S(2)}) copy-start(f32[2880]{0:T(1024)} %param.28) | copy-start | bytes 34564
  246.4 245.7 %reduce-scatter.4.cloned.1.call-start = ((), (), s32[]{:S(2)}) async-start(), calls=%async_computation.8 | async-start | bytes 3317760
  321.9 0.8 copy-start.3
  380.2 1.6 copy-start.2
  455.4 0.9 copy-start.19
  455.4 1.0 copy-start.8
  455.4 24.3 %copy-start.18 = (s32[32]{0:T(128)S(1)}, s32[32]{0:T(128)}, u32[]{:S(2)}) copy-start(s32[32]{0:T(128)} %param.35) | copy-start | bytes 388
  479.8 33.0 %copy-start.17 = (f32[64,4]{0,1:T(4,128)S(1)}, f32[64,4]{0,1:T(4,128)}, u32[]{:S(2)}) copy-start(f32[64,4]{0,1:T(4,128)} %param.30) | copy-start | bytes 3076
  501.6 21.3 %all-to-all-start.4 = ((bf16[32,16,360]{2,1,0:T(8,128)(2,1)}), bf16[32,16,360]{2,1,0:T(8,128)(2,1)S(1)}, u32[]{:S(2)}, u32[]{:S(2)}) async-start(bf16[32,16,360]{2,1,0:T(8,128)(2,1)} %copy.109), calls=%async_computation.4 | async-start | bytes 786432 | tf_op jit(solution)/shard_map/all_to_all | solution.py:195
Sparse Core Ops, SparseCore 0:
  10.6 53.0 all-gather.2
  246.5 73.8 all-reduce.2
  455.6 36.5 reduce-scatter.3
where the time goes:
time: 536 us; the launch traced here: 533 us
  local copies, waits for them, and re-layouts  164 us (31%)
  waiting for transfers between devices  158 us (29%)
  blocking collectives  96.2 us (18%)
  matrix products  42.4 us (8%)
  other arithmetic  32.4 us (6%)
  starting transfers between devices  25 us (5%)
  between operations  14.9 us (3%)
    unnamed x48, local copies, waits for them, and re-layouts  77 us
    psum x1, waiting for transfers between devices, shards(): summed = lax.psum(projected, 'tp')  72.6 us
    all_gather x1, waiting for transfers between devices, shards(): every_query = lax.all_gather(queries, 'seq', axis=0, tiled=True)  53.3 us
    all_to_all x1, blocking collectives, shards(): lax.all_to_all(dispatched, 'seq', split_axis=0, concat_axis=0, tiled=True)  50.3 us
    all_gather x1, blocking collectives, shards(): resid_full = lax.all_gather(hidden_in, 'tp', axis=1, tiled=True)  23.3 us
    all_gather x1, blocking collectives, shards(): everyone = lax.all_gather(picked_rows, 'seq', axis=0, tiled=True)  22.6 us
    gather x8, local copies, waits for them, and re-layouts, cache_block(): picked = jnp.take(cache_kv, block_groups, axis=0)  20.7 us
    mul x3, local copies, waits for them, and re-layouts, shards(): shard_scale[..., None]  14.9 us
  transfers between devices with their start and end apart: 7, of which 6 were waited for; matrix products, arithmetic and copies ran while one was open for 7% of the time, Pallas kernels for 0%

commit v1 on v0

--- a/solution.py
+++ b/solution.py
@@ -154,7 +154,7 @@
     projected = jnp.dot(attention, w_out, preferred_element_type=jnp.float32)
     width_dev = hidden_in.shape[1]
     tp_index = lax.axis_index("tp")
-    summed = lax.psum(projected, "tp")
+    summed = jnp.sum(lax.all_gather(projected, "tp"), axis=0)
     resid_full = lax.all_gather(hidden_in, "tp", axis=1, tiled=True)
     stream = (resid_full.astype(jnp.float32) + summed).astype(jnp.bfloat16)
     stream_f = stream.astype(jnp.float32)

time: 536 us -> 513 us (0.957)
  waiting for transfers between devices: 158 us -> 138 us
  blocking collectives: 96.2 us -> 90.5 us
    psum x1 -> x0, waiting for transfers between devices: 72.6 us -> none  [shards(): summed = lax.psum(projected, 'tp')]
    all_gather x0 -> x1, waiting for transfers between devices: none -> 45.5 us  [shards(): summed = jnp.sum(lax.all_gather(projected, 'tp'), axis=0)]
    unnamed x48 -> x42, local copies, waits for them, and re-layouts: 77 us -> 77.5 us
  transfers between devices with their start and end apart: 7 -> 7, of which waited for: 6 -> 7; matrix products, arithmetic and copies ran while one was open for 7% -> 7% of each run, Pallas kernels for 0% -> 0%
where the time goes in v1:
time: 513 us; the launch traced here: 510 us
  local copies, waits for them, and re-layouts  164 us (32%)
  waiting for transfers between devices  138 us (27%)
  blocking collectives  90.5 us (18%)
  matrix products  40.9 us (8%)
  other arithmetic  37.2 us (7%)
  starting transfers between devices  25.3 us (5%)
  between operations  14.8 us (3%)
    unnamed x42, local copies, waits for them, and re-layouts  77.5 us
    all_gather x1, waiting for transfers between devices, shards(): every_query = lax.all_gather(queries, 'seq', axis=0, tiled=True)  54.9 us
    all_gather x1, waiting for transfers between devices, shards(): summed = jnp.sum(lax.all_gather(projected, 'tp'), axis=0)  45.5 us
    all_to_all x1, blocking collectives, shards(): lax.all_to_all(dispatched, 'seq', split_axis=0, concat_axis=0, tiled=True)  45.1 us
    all_gather x1, blocking collectives, shards(): resid_full = lax.all_gather(hidden_in, 'tp', axis=1, tiled=True)  22.7 us
    all_gather x1, blocking collectives, shards(): everyone = lax.all_gather(picked_rows, 'seq', axis=0, tiled=True)  22.6 us
    gather x8, local copies, waits for them, and re-layouts, cache_block(): picked = jnp.take(cache_kv, block_groups, axis=0)  20.7 us
    mul x3, local copies, waits for them, and re-layouts, shards(): shard_scale[..., None]  14.9 us
  transfers between devices with their start and end apart: 7, of which 7 were waited for; matrix products, arithmetic and copies ran while one was open for 7% of the time, Pallas kernels for 0%

profile of v1, /device:TPU:1, one launch (start us, length us, event | category | flops | bytes accessed | tf_op | source)
XLA Modules:
  0.0 510.2 jit_solution(799353927532771245)
XLA Ops:
  8.8 54.9 %all-gather.5.cloned.1.call-done = bf16[32,64,512]{2,1,0:T(8,128)(2,1)} async-done(((bf16[1,64,512]{2,1,0:T(8,128)(2,1)}), bf16[32,64,512]{2,1,0:T(8,128)(2,1)}) %all-gather.5.cloned.1.call-update) | async-done | bytes 2097168 | tf_op jit(solution)/shard_map/all_gather | solution.py:96
  63.7 97.3 %while.15 = (s32[]{:T(128)}, bf16[4,8,64,512]{3,2,1,0:T(8,128)(2,1)}, f32[4,8,64,8]{2,3,1,0:T(8,128)}, f32[4,8,64,8]{2,3,1,0:T(8,128)}, s32[4,8]{1,0:T(4,128)S(1...) while((s32[]{:T(128)}, ...), condition=%wide.region_3.4_spmd.clone, body=%wide.region_0.3_spmd.clone.sunk | while | flops 565184128 | bytes 43791872 | solution.py:103
  65.0 2.9 gather_fusion.1
  67.9 2.3 copy.146
  70.2 2.4 bitcast_select_fusion.4
  75.3 2.7 bitcast_reduce_fusion.3
  78.0 2.3 fusion.128
  80.9 2.6 fusion.129
  83.5 1.7 copy.147
  85.2 1.9 broadcast_in_dim.201
  89.3 2.9 gather_fusion.1
  92.2 2.3 copy.146
  94.5 2.4 bitcast_select_fusion.4
  99.6 2.7 bitcast_reduce_fusion.3
  102.3 2.3 fusion.128
  105.2 2.6 fusion.129
  107.9 1.7 copy.147
  109.6 1.9 broadcast_in_dim.201
  113.7 2.9 gather_fusion.1
  116.6 2.3 copy.146
  118.9 2.4 bitcast_select_fusion.4
  123.9 2.7 bitcast_reduce_fusion.3
  126.6 2.3 fusion.128
  129.6 2.6 fusion.129
  132.2 1.7 copy.147
  133.9 1.9 broadcast_in_dim.201
  138.0 2.9 gather_fusion.1
  140.9 2.3 copy.146
  143.2 2.4 bitcast_select_fusion.4
  148.2 2.7 bitcast_reduce_fusion.3
  150.9 2.3 fusion.128
  153.9 2.6 fusion.129
  156.5 1.7 copy.147
  158.2 1.9 broadcast_in_dim.201
  161.0 1.7 reshape.755
  162.7 5.1 all-to-all-start.1
  168.7 1.7 reshape.753
  170.3 4.7 all-to-all-done.1
  175.1 3.9 all-to-all-start
  179.1 7.3 %all-to-all-done = f32[32,1,512]{2,1,0:T(1,128)S(1)} async-done(((f32[32,1,512]{2,1,0:T(1,128)}), f32[32,1,512]{2,1,0:T(1,128)S(1)}, u32[]{:S(2)}, u32[]{:S(2)}) %all-to-all-start) | async-done | bytes 65568 | tf_op jit(solution)/shard_map/all_to_all | solution.py:112
  186.4 4.7 all-to-all-start.2
  196.5 1.6 reduce.11
  202.7 5.9 %mul.135 = f32[32,64,8,64]{3,2,1,0:T(8,128)} broadcast(f32[32,64,8]{2,1,0:T(8,128)} %copy.109), dimensions={0,1,2} | broadcast | bytes 4259840 | tf_op jit(solution)/shard_map/mul | solution.py:144
  208.6 7.5 %mul.136 = f32[32,1,64,512]{3,2,1,0:T(8,128)} reshape(f32[32,64,8,64]{3,2,1,0:T(8,128)} %mul.135) | data formatting | bytes 8388608 | tf_op jit(solution)/shard_map/mul | solution.py:144
  216.1 3.0 all-to-all-done.2
  219.1 3.5 multiply_reduce_fusion
  222.7 1.9 fusion.77
  225.0 22.7 %all-gather.1 = bf16[8,360,64]{1,2,0:T(8,128)(2,1)S(1)} all-gather(bf16[1,360,64]{1,2,0:T(8,128)(2,1)S(1)} %bitcast.320), channel_id=1, replica_groups=mesh['seq'=32,'tp'=8] {'tp'}, dimensions={0}, use_global_device_ids=true | all-gather | bytes 414720 | tf_op jit(solution)/shard_map/all_gather | solution.py:158
  248.9 2.3 reshape.729
  252.4 45.5 %all-gather.7.cloned.1.call-done = f32[512,2880]{1,0:T(8,128)} async-done(((f32[64,2880]{1,0:T(8,128)}), f32[512,2880]{1,0:T(8,128)}) %all-gather.7.cloned.1.call-update) | async-done | bytes 5898256 | tf_op jit(solution)/shard_map/all_gather | solution.py:157
  297.9 4.0 reduce_sum.93
  304.2 2.7 convolution_convert_fusion.1
  306.8 4.6 copy.120
  311.4 45.1 %all_to_all.25 = bf16[32,16,2880]{2,1,0:T(8,128)(2,1)S(1)} all-to-all(bf16[32,16,2880]{2,1,0:T(8,128)(2,1)} %bitcast.310), channel_id=1, replica_groups=mesh['seq'=32,'tp'=8] {'seq'}, dimensions={0} | all-to-all | bytes 5898240 | tf_op jit(solution)/shard_map/all_to_all | solution.py:188
  358.1 4.2 fusion.27
  362.4 8.5 %convolution_convert_fusion = bf16[32,16,2880]{2,1,0:T(8,128)(2,1)} fusion(bf16[1,360,2880]{2,1,0:T(8,128)(2,1)} %param.32, bf16[32,16,2880]{2,1,0:T(8,128)(2,1)} %copy-done.2, bf16[1,2,2880,360]{2,3,1,0:T(8,128)(2,1)} %param.31, f32[32,1,16,360]{3,2,0,1:T(8,128)} %fusion.27), kind=kOutput, calls=%fused_computation.40 | convolution fusion | flops 2126315520 | bytes 10989568 | tf_op jit(solution)/shard_map/sexf,efd->sexd/dot_general | solution.py:66
  370.9 21.4 %copy.125 = bf16[32,16,2880]{1,0,2:T(8,128)(2,1)} copy(bf16[32,16,2880]{2,1,0:T(8,128)(2,1)} %convolution_convert_fusion) | data formatting | bytes 5898240
  392.2 39.5 %reshape.750 = bf16[2880,512]{1,0:T(8,128)(2,1)} reshape(bf16[2880,32,16]{2,1,0:T(8,128)(2,1)} %bitcast.307) | data formatting | bytes 5898240
  433.4 22.6 %all_gather.19 = bf16[32,16,1,128]{3,1,2,0:T(8,128)(2,1)S(1)} all-gather(bf16[1,16,1,128]{3,1,2,0:T(8,128)(2,1)S(1)} %bitcast_select_fusion.2), channel_id=1, replica_groups=mesh['seq'=32,'tp'=8] {'seq'}, dimensions={0}, use_global_device_ids=true | all-gather | bytes 135168 | tf_op jit(solution)/shard_map/all_gather | solution.py:205
  456.1 12.7 %reduce-scatter.4.cloned.1.call-done = bf16[360,512]{1,0:T(8,128)(2,1)} async-done(((bf16[2880,512]{1,0:T(8,128)(2,1)}), bf16[360,512]{1,0:T(8,128)(2,1)}) %reduce-scatter.4.cloned.1.call-update) | async-done | bytes 368656
  468.8 4.4 reshape.751
  473.2 5.0 copy.126
  478.2 11.3 %all-to-all-start.4 = ((bf16[32,16,360]{2,1,0:T(8,128)(2,1)}), bf16[32,16,360]{2,1,0:T(8,128)(2,1)S(1)}, u32[]{:S(2)}, u32[]{:S(2)}) async-start(bf16[32,16,360]{2,1,0:T(8,128)(2,1)} %copy.126), calls=%async_computation.4 | async-start | bytes 786432 | tf_op jit(solution)/shard_map/all_to_all | solution.py:195
  491.0 8.7 %all-to-all-done.4 = bf16[32,16,360]{2,1,0:T(8,128)(2,1)S(1)} async-done(((bf16[32,16,360]{2,1,0:T(8,128)(2,1)}), bf16[32,16,360]{2,1,0:T(8,128)(2,1)S(1)}, u32[]{:S(2)}, u32[]{:S(2)}) %all-to-all-start.4) | async-done | bytes 368672 | tf_op jit(solution)/shard_map/all_to_all | solution.py:195
  (157 shorter events, 47.5 us)
Async XLA Ops:
  7.2 215.5 %copy-start = (bf16[512,2880]{0,1:T(8,128)(2,1)S(1)}, bf16[512,2880]{0,1:T(8,128)(2,1)}, u32[]{:S(2)}) copy-start(bf16[512,2880]{0,1:T(8,128)(2,1)} %param.26) | copy-start | bytes 8847364
  7.2 56.5 %all-gather.5.cloned.1.call-start = ((), (), s32[]{:S(2)}) async-start(), calls=%async_computation.6 | async-start | bytes 2162688 | tf_op jit(solution)/shard_map/all_gather | solution.py:96
  78.0 3.0 copy-start.1
  102.3 3.0 copy-start.1
  126.6 3.0 copy-start.1
  150.9 3.0 copy-start.1
  161.0 30.6 %copy-start.6 = (bf16[1,64,512]{2,1,0:T(8,128)(2,1)S(1)}, bf16[1,64,512]{2,1,0:T(8,128)(2,1)}, u32[]{:S(2)}) copy-start(bf16[1,64,512]{2,1,0:T(8,128)(2,1)} %param.19) | copy-start | bytes 196612
  161.0 31.3 %copy-start.7 = (bf16[1,64,1,128]{3,1,2,0:T(8,128)(2,1)S(1)}, bf16[1,64,1,128]{3,1,2,0:T(8,128)(2,1)}, u32[]{:S(2)}) copy-start(bf16[1,64,1,128]{3,1,2,0:T(8,128)(2,1)} %param.20) | copy-start | bytes 49156
  162.7 12.4 %all-to-all-start.1 = ((f32[32,1,512]{2,1,0:T(1,128)}), f32[32,1,512]{2,1,0:T(1,128)S(1)}, u32[]{:S(2)}, u32[]{:S(2)}) async-start(f32[32,1,512]{2,1,0:T(1,128)} %reshape.755), calls=%async_computation.1 | async-start | bytes 131072 | tf_op jit(solution)/shard_map/all_to_all | solution.py:111
  175.1 11.3 %all-to-all-start = ((f32[32,1,512]{2,1,0:T(1,128)}), f32[32,1,512]{2,1,0:T(1,128)S(1)}, u32[]{:S(2)}, u32[]{:S(2)}) async-start(f32[32,1,512]{2,1,0:T(1,128)} %reshape.753), calls=%async_computation | async-start | bytes 131072 | tf_op jit(solution)/shard_map/all_to_all | solution.py:112
  186.4 5.8 %copy-start.8 = (f32[32,1,512]{2,1,0:T(1,128)}, f32[32,1,512]{2,1,0:T(1,128)S(1)}, u32[]{:S(2)}) copy-start(f32[32,1,512]{2,1,0:T(1,128)S(1)} %all-to-all-done) | copy-start | bytes 196612
  186.4 32.7 %all-to-all-start.2 = ((bf16[32,1,64,512]{3,2,1,0:T(8,128)(2,1)}), bf16[32,1,64,512]{3,2,1,0:T(8,128)(2,1)}, u32[]{:S(2)}, u32[]{:S(2)}) async-start(bf16[32,1,64,512]{3,2,1,0:T(8,128)(2,1)} %bitcast.315), calls=%async_computation.2 | async-start | bytes 4194304 | tf_op jit(solution)/shard_map/all_to_all | solution.py:109
  191.1 106.8 %all-gather.7.cloned.1.call-start = ((), (), s32[]{:S(2)}) async-start(), calls=%async_computation.7 | async-start | bytes 6782976 | tf_op jit(solution)/shard_map/all_gather | solution.py:157
  192.3 0.6 copy-start.9
  192.6 0.6 copy-start.10
  216.1 6.6 %copy-start.4 = (f32[64,512]{1,0:T(8,128)S(1)}, f32[64,512]{1,0:T(8,128)}, u32[]{:S(2)}) copy-start(f32[64,512]{1,0:T(8,128)} %reshape.677) | copy-start | bytes 393220
  216.1 6.6 %copy-start.5 = (f32[64,512]{1,0:T(8,128)S(1)}, f32[64,512]{1,0:T(8,128)}, u32[]{:S(2)}) copy-start(f32[64,512]{1,0:T(8,128)} %mul.139) | copy-start | bytes 393220
  222.7 2.0 copy-start.12
  222.7 2.3 copy-start.11
  224.6 244.2 %reduce-scatter.4.cloned.1.call-start = ((), (), s32[]{:S(2)}) async-start(), calls=%async_computation.8 | async-start | bytes 3317760
  297.9 6.3 %copy-start.13 = (f32[2880]{0:T(1024)S(1)}, f32[2880]{0:T(1024)}, u32[]{:S(2)}) copy-start(f32[2880]{0:T(1024)} %param.28) | copy-start | bytes 34564
  303.4 0.8 copy-start.3
  356.5 1.6 copy-start.2
  431.7 0.9 copy-start.16
  431.7 24.2 %copy-start.15 = (s32[32]{0:T(128)S(1)}, s32[32]{0:T(128)}, u32[]{:S(2)}) copy-start(s32[32]{0:T(128)} %param.35) | copy-start | bytes 388
  456.1 33.5 %copy-start.14 = (f32[64,4]{0,1:T(4,128)S(1)}, f32[64,4]{0,1:T(4,128)}, u32[]{:S(2)}) copy-start(f32[64,4]{0,1:T(4,128)} %param.30) | copy-start | bytes 3076
  478.2 21.5 %all-to-all-start.4 = ((bf16[32,16,360]{2,1,0:T(8,128)(2,1)}), bf16[32,16,360]{2,1,0:T(8,128)(2,1)S(1)}, u32[]{:S(2)}, u32[]{:S(2)}) async-start(bf16[32,16,360]{2,1,0:T(8,128)(2,1)} %copy.126), calls=%async_computation.4 | async-start | bytes 786432 | tf_op jit(solution)/shard_map/all_to_all | solution.py:195
Sparse Core Ops, SparseCore 0:
  10.6 53.0 all-gather.4
  224.8 73.0 all-gather.6
  431.9 36.8 reduce-scatter.3
